TPU v7x, 32 devices: a whole 2x2x4 slice. The times are simulated.
32 devices in a mesh: groups: 2 (over x), tm: 8 (over z, y), rows: 2 (over core).
Axes of the slice: x: 2, y: 2, z: 4, core: 2. Of those that a mesh axis runs over, the one named last changes fastest.
Arguments:
- iterate: float32 [32, 512, 512], P(('groups', 'tm'), 'rows'), parts along dimension 0, may hold values from -6 to 6
- forcing: float32 [32, 512, 512], P(('groups', 'tm'), 'rows'), parts along dimension 0, may hold values from -18 to 18
- initial_state: float32 [1024, 512], P(('groups', 'rows')), parts along dimension 0, may hold values from -6 to 6
- diffusivity: float32 [1024, 512], P(('groups', 'rows')), parts along dimension 0, may hold values from 0.5 to 4
Outputs:
- updated: float32 [32, 512, 512], P(('groups', 'tm'), 'rows'), parts along dimension 0
- residual_rms: float32 [32], P(('groups', 'tm')), parts along dimension 0
There are 2 independent parts, one for each index of `groups`. A program takes and returns all parts, laid end to end along the dimension named above; each array names one. Nothing has to cross between parts.
All inputs are finite; a program needn't handle non-finite values.
Results may differ from a plain program's by a relative error of at most 0.0003.
Values sent between devices are 32-bit elements; how exact they have to be, the bound alone decides.
No kernel may reach another device: no remote copies, remote signals or barrier semaphores. Data moves between devices by JAX's collectives and lax.ppermute only.
A program may use at most 64 MiB of HBM per device.

v0:
```python
import jax
import jax.numpy as jnp
from jax import lax
from jax.sharding import PartitionSpec as P

CG_ITERS = 3
circulant_alpha = 0.05
time_step = 0.5
rms_eps = 1e-06


def extended(block, sides, width):
    for axis, dim in sides:
        count = lax.axis_size(axis)
        forward = [(i, i + 1) for i in range(count - 1)]
        backward = [(target, source) for source, target in forward]
        low = lax.ppermute(
            lax.slice_in_dim(block, block.shape[dim] - width, None, axis=dim), axis, forward
        )
        high = lax.ppermute(lax.slice_in_dim(block, 0, width, axis=dim), axis, backward)
        block = jnp.concatenate([low, block, high], axis=dim)
    return block


def from_behind(value, axis, steps):
    count = lax.axis_size(axis)
    initial, last = (max(0, -steps), min(count, count - steps))
    return lax.ppermute(value, axis, [(source, source + steps) for source in range(initial, last)])


def phase_table(first_index, second_index, length):
    product = first_index[:, None] * second_index[None, :] % length
    return 2.0 * jnp.pi / length * product.astype(jnp.float32)


def faces_from(padded_rows):
    centre = padded_rows[1:-1]
    columns = jnp.pad(centre, ((0, 0), (1, 1)), mode="edge")
    north_face = 0.5 * (centre + padded_rows[:-2])
    south_face = 0.5 * (centre + padded_rows[2:])
    west_face = 0.5 * (centre + columns[:, :-2])
    east_face = 0.5 * (centre + columns[:, 2:])
    return (north_face, south_face, west_face, east_face)


def apply_faces(padded_rows, weights):
    north_face, south_face, west_face, east_face = weights
    centre = padded_rows[..., 1:-1, :]
    lead_pad = [(0, 0)] * (centre.ndim - 1)
    columns = jnp.pad(centre, lead_pad + [(1, 1)])
    return (
        (north_face + south_face + west_face + east_face) * centre
        - north_face * padded_rows[..., :-2, :]
        - south_face * padded_rows[..., 2:, :]
        - west_face * columns[..., :-2]
        - east_face * columns[..., 2:]
    )


def high_dot(first_mat, second_mat):
    return jnp.dot(
        first_mat, second_mat, precision=lax.Precision.HIGHEST, preferred_element_type=jnp.float32
    )


def shards(iterate, forcing, initial_state, diffusivity):
    steps_dev, rows_dev, columns_dev = iterate.shape
    time_devices = lax.axis_size("tm")
    row_devices = lax.axis_size("rows")
    time_rank = lax.axis_index("tm")
    row_rank = lax.axis_index("rows")
    length = steps_dev * time_devices
    cell_count = rows_dev * row_devices * columns_dev
    rimmed = extended(diffusivity, (("rows", 0),), 1)
    top_row = jnp.where(row_rank == 0, diffusivity[:1], rimmed[:1])
    bottom_row = jnp.where(row_rank == row_devices - 1, diffusivity[-1:], rimmed[-1:])
    rimmed = jnp.concatenate([top_row, rimmed[1:-1], bottom_row], axis=0)
    local_faces = faces_from(rimmed)
    arriving = from_behind(iterate[-1], "tm", 1)
    first_previous = jnp.where(time_rank == 0, initial_state, arriving)
    previous = jnp.concatenate([first_previous[None], iterate[:-1]], axis=0)
    iterate_rim = extended(iterate, (("rows", 1),), 1)
    residual = (
        time_step * forcing + previous - iterate - time_step * apply_faces(iterate_rim, local_faces)
    )
    squares = lax.psum(jnp.sum(residual * residual, axis=(1, 2)), "rows")
    residual_rms = jnp.sqrt(squares / cell_count + rms_eps)
    step_index = time_rank * steps_dev + jnp.arange(steps_dev, dtype=jnp.int32)
    log_alpha = jnp.log(jnp.float32(circulant_alpha))
    growth = jnp.exp(log_alpha * step_index.astype(jnp.float32) / length)
    scaled = residual * growth[:, None, None]
    by_cells = lax.all_to_all(scaled, "tm", split_axis=1, concat_axis=0, tiled=True)
    slab_rows = by_cells.shape[1]
    all_index = jnp.arange(length, dtype=jnp.int32)
    angles = phase_table(all_index, all_index, length)
    flat_cells = by_cells.reshape(length, slab_rows * columns_dev)
    spectrum_real = high_dot(jnp.cos(angles), flat_cells)
    spectrum_imag = high_dot(-jnp.sin(angles), flat_cells)
    spectrum = jnp.stack([spectrum_real, spectrum_imag]).reshape(2, length, slab_rows, columns_dev)
    by_freq = lax.all_to_all(spectrum, "tm", split_axis=1, concat_axis=2, tiled=True)
    freq_index = time_rank * steps_dev + jnp.arange(steps_dev, dtype=jnp.int32)

    def rim_rows(values):
        return extended(values, (("rows", 2),), 1)

    def reduce_sums(values):
        return lax.psum(values, "rows")

    root_alpha = jnp.exp(log_alpha / length)
    freq_angle = 2.0 * jnp.pi / length * freq_index.astype(jnp.float32)
    real_shift = (1.0 - root_alpha * jnp.cos(freq_angle))[:, None, None]
    imag_shift = (root_alpha * jnp.sin(freq_angle))[:, None, None]

    def operate(values, orientation):
        spread = time_step * apply_faces(rim_rows(values), local_faces)
        swapped = jnp.stack([-values[1], values[0]])
        return real_shift * values + orientation * imag_shift * swapped + spread

    def freq_norm(values):
        return jnp.sum(values * values, axis=(0, 2, 3))

    def expand(values):
        return values[None, :, None, None]

    solution = jnp.zeros_like(by_freq)
    normal = operate(by_freq, -1.0)
    gamma_now = reduce_sums(freq_norm(normal))
    search = normal
    remain = by_freq
    for iteration in range(CG_ITERS):
        image_now = operate(search, 1.0)
        step_rate = gamma_now / reduce_sums(freq_norm(image_now))
        solution = solution + expand(step_rate) * search
        if iteration + 1 < CG_ITERS:
            remain = remain - expand(step_rate) * image_now
            normal = operate(remain, -1.0)
            gamma_next = reduce_sums(freq_norm(normal))
            search = normal + expand(gamma_next / gamma_now) * search
            gamma_now = gamma_next
    back_cells = lax.all_to_all(solution, "tm", split_axis=2, concat_axis=1, tiled=True)
    inverse_angles = phase_table(all_index, all_index, length)
    flat_real = back_cells[0].reshape(length, slab_rows * columns_dev)
    flat_imag = back_cells[1].reshape(length, slab_rows * columns_dev)
    correction = high_dot(jnp.cos(inverse_angles) / length, flat_real) - high_dot(
        jnp.sin(inverse_angles) / length, flat_imag
    )
    correction = correction.reshape(length, slab_rows, columns_dev)
    own_steps = lax.all_to_all(correction, "tm", split_axis=0, concat_axis=1, tiled=True)
    updated = iterate + own_steps / growth[:, None, None]
    return (updated, residual_rms)


def solution(mesh):
    placed = (
        P(("groups", "tm"), "rows", None),
        P(("groups", "tm"), "rows", None),
        P(("groups", "rows"), None),
        P(("groups", "rows"), None),
    )
    return jax.shard_map(
        shards,
        mesh=mesh,
        in_specs=placed,
        out_specs=(P(("groups", "tm"), "rows", None), P(("groups", "tm"))),
        check_vma=False,
    )
```

profile of v0, /device:TPU:0, one launch (start us, length us, event | category | flops | bytes accessed | tf_op | source)
XLA Modules:
  0.0 287.9 jit_solution(17938583159256987728)
XLA Ops:
  3.5 3.0 %collective-permute-start.3 = (f32[2,1,512]{2,1,0:T(1,128)S(1)}, f32[2,1,512]{2,1,0:T(1,128)S(1)}, u32[]{:S(2)}, u32[]{:S(2)}) collective-permute-start(f32[2,1,512]{2,1,0:T(1,128)S(1)} %get-tuple-element.53), channel_id=1, source_target_pairs={{0,1},{2,3},{4,5},{6,7},{8,9},{10,11},{12,13},{14,15},{16,17},{18,... | collective-permute-start | bytes 12296 | tf_op jit(solution)/shard_map/ppermute | solution.py:17
  7.8 2.1 slice_bitcast_fusion
  9.9 5.1 %collective-permute-start = (f32[256,512]{1,0:T(8,128)}, f32[256,512]{1,0:T(8,128)S(1)}, u32[]{:S(2)}, u32[]{:S(2)}) collective-permute-start(f32[256,512]{1,0:T(8,128)} %get-tuple-element.51), channel_id=1, source_target_pairs={{0,2},{2,4},{4,6},{6,8},{8,10},{10,12},{12,14},{1,3},{3,5},{5,7},{... | collective-permute-start | bytes 1572872 | tf_op jit(solution)/shard_map/ppermute | solution.py:28
  15.1 2.7 collective-permute-start.1
  19.1 8.3 %collective-permute-done = f32[256,512]{1,0:T(8,128)S(1)} collective-permute-done((f32[256,512]{1,0:T(8,128)}, f32[256,512]{1,0:T(8,128)S(1)}, u32[]{:S(2)}, u32[]{:S(2)}) %collective-permute-start) | collective-permute-done | bytes 524320 | tf_op jit(solution)/shard_map/ppermute | solution.py:28
  29.6 32.5 %all_to_all.66 = f32[2,256,512]{2,0,1:T(2,128)S(1)} all-to-all(f32[2,256,512]{2,0,1:T(2,128)S(1)} %copy.31), channel_id=1, replica_groups=mesh['groups'=2,'tm'=8,'rows'=2] {'tm'}, dimensions={1} | all-to-all | bytes 2097152 | tf_op jit(solution)/shard_map/all_to_all | solution.py:92
  62.3 1.5 convolution_bitcast_fusion
  63.8 1.5 convolution_bitcast_fusion.1
  65.7 2.6 copy.35
  68.2 3.6 %all-to-all-start.1 = ((f32[2,16,32,512]{3,2,0,1:T(8,128)}), f32[2,16,32,512]{3,2,0,1:T(8,128)S(1)}, u32[]{:S(2)}, u32[]{:S(2)}) async-start(f32[2,16,32,512]{3,2,0,1:T(8,128)} %copy.35), calls=%async_computation.1 | async-start | bytes 4194304 | tf_op jit(solution)/shard_map/all_to_all | solution.py:100
  72.0 47.8 %all-to-all-done.1 = f32[2,16,32,512]{3,2,0,1:T(8,128)S(1)} async-done(((f32[2,16,32,512]{3,2,0,1:T(8,128)}), f32[2,16,32,512]{3,2,0,1:T(8,128)S(1)}, u32[]{:S(2)}, u32[]{:S(2)}) %all-to-all-start.1) | async-done | bytes 2097184 | tf_op jit(solution)/shard_map/all_to_all | solution.py:100
  121.3 1.3 collective-permute-start.6
  124.6 2.5 multiply_reduce_fusion.4
  127.1 3.0 %collective-permute-start.7 = (f32[2,2,1,512]{3,2,1,0:T(1,128)S(1)}, f32[2,2,1,512]{3,2,1,0:T(1,128)S(1)}, u32[]{:S(2)}, u32[]{:S(2)}) collective-permute-start(f32[2,2,1,512]{3,2,1,0:T(1,128)S(1)} %get-tuple-element.45), channel_id=1, source_target_pairs={{0,1},{2,3},{4,5},{6,7},{8,9},{10,11},{12,13},{14,15},{16,17},{18,... | collective-permute-start | bytes 24584 | tf_op jit(solution)/shard_map/ppermute | solution.py:17
  130.1 1.5 collective-permute-start.8
  131.9 1.3 collective-permute-done.8
  133.2 3.4 %multiply_reduce_fusion.3 = (f32[2]{0:T(128)S(1)}, f32[2,2,256,512]{3,2,1,0:T(8,128)}) fusion(f32[256,512]{1,0:T(8,128)S(1)} %copy-done.15, f32[2,2,256,512]{3,2,1,0:T(8,128)S(1)} %get-tuple-element.19, f32[256,512]{1,0:T(8,128)S(1)} %copy-done.9, f32[2,2,1,512]{3,2,1,0:T(1,128)S(1)} %collective-permute-done.8, f32[256,512]{1,0:T(8,128)S(1)} %copy-done.3, ...), kind=kLoop, calls=%fused_computation.109 | loop fusion | flops 9961470 | bytes 8929304 | tf_op jit(solution)/shard_map/reduce_sum | solution.py:120
  136.6 2.4 all-reduce.8
  139.1 2.8 multiply_subtract_fusion.1
  141.9 2.1 collective-permute-start.9
  144.0 1.4 collective-permute-start.10
  145.7 1.5 collective-permute-done.10
  147.2 3.5 %multiply_reduce_fusion.2 = (f32[2]{0:T(128)S(1)}, f32[2,2,256,512]{3,2,1,0:T(8,128)}) fusion(f32[256,512]{1,0:T(8,128)S(1)} %copy-done.16, f32[2,2,256,512]{3,2,1,0:T(8,128)S(1)} %multiply_subtract_fusion.1, f32[256,512]{1,0:T(8,128)S(1)} %copy-done.10, f32[2,2,1,512]{3,2,1,0:T(1,128)S(1)} %collective-permute-done.10, f32[256,512]{1,0:T(8,128)S(1)} %copy-done.4, ...), kind=kLoop, calls=%fused_computation.107 | loop fusion | flops 9961470 | bytes 8929304 | tf_op jit(solution)/shard_map/reduce_sum | solution.py:120
  150.7 2.4 psum.51
  153.2 2.1 multiply_add_fusion.2
  155.4 2.1 collective-permute-start.11
  157.5 1.4 collective-permute-start.12
  159.2 1.5 collective-permute-done.12
  160.7 3.5 %multiply_reduce_fusion.1 = (f32[2]{0:T(128)S(1)}, f32[2,2,256,512]{3,2,1,0:T(8,128)}) fusion(f32[256,512]{1,0:T(8,128)S(1)} %copy-done.17, f32[2,2,256,512]{3,2,1,0:T(8,128)S(1)} %multiply_add_fusion.2, f32[256,512]{1,0:T(8,128)S(1)} %copy-done.11, f32[2,2,1,512]{3,2,1,0:T(1,128)S(1)} %collective-permute-done.12, f32[256,512]{1,0:T(8,128)S(1)} %copy-done.5, ...), kind=kLoop, calls=%fused_computation.105 | loop fusion | flops 9961470 | bytes 8929304 | tf_op jit(solution)/shard_map/reduce_sum | solution.py:120
  164.2 2.4 psum.52
  166.7 2.8 multiply_subtract_fusion
  169.5 2.1 collective-permute-start.13
  171.6 1.4 collective-permute-start.14
  173.3 1.5 collective-permute-done.14
  174.8 3.5 %multiply_reduce_fusion = (f32[2]{0:T(128)S(1)}, f32[2,2,256,512]{3,2,1,0:T(8,128)}) fusion(f32[256,512]{1,0:T(8,128)S(1)} %copy-done.18, f32[2,2,256,512]{3,2,1,0:T(8,128)S(1)} %multiply_subtract_fusion, f32[256,512]{1,0:T(8,128)S(1)} %copy-done.12, f32[2,2,1,512]{3,2,1,0:T(1,128)S(1)} %collective-permute-done.14, f32[256,512]{1,0:T(8,128)S(1)} %copy-done.6, ...), kind=kLoop, calls=%fused_computation.103 | loop fusion | flops 9961470 | bytes 8929304 | tf_op jit(solution)/shard_map/reduce_sum | solution.py:120
  178.3 2.4 psum.53
  180.8 2.8 multiply_add_fusion.1
  183.6 2.1 collective-permute-start.15
  185.7 1.4 collective-permute-start.16
  187.4 1.5 collective-permute-done.16
  188.9 2.5 fusion.36
  191.4 2.7 all-reduce.7
  194.0 3.1 %multiply_add_fusion = f32[2,2,256,512]{3,2,1,0:T(8,128)S(1)} fusion(f32[2,2,256,512]{3,2,1,0:T(8,128)} %copy-done, f32[2,2,256,512]{3,2,1,0:T(8,128)S(1)} %get-tuple-element.19, f32[2]{0:T(128)S(1)} %div.42, f32[2]{0:T(128)S(1)} %div.40, f32[2]{0:T(128)S(1)} %div.38, f32[2,2,256,512]{3,2,1,0:T(8,128)} %get-tuple-element.11, f32[2]{0:T(128)S(1)} %div.41), kind=kLoop, calls=%fused_computation.101 | loop fusion | flops 3670016 | bytes 8388640 | tf_op jit(solution)/shard_map/add | solution.py:133
  197.1 1.6 copy.40
  198.7 52.6 %all_to_all.67 = f32[2,2,256,512]{3,1,0,2:T(2,128)S(1)} all-to-all(f32[2,2,256,512]{3,1,0,2:T(2,128)S(1)} %copy.40), channel_id=1, replica_groups=mesh['groups'=2,'tm'=8,'rows'=2] {'tm'}, dimensions={2} | all-to-all | bytes 4194304 | tf_op jit(solution)/shard_map/all_to_all | solution.py:140
  255.6 1.6 copy.48
  257.2 3.8 %all-to-all-start.3 = ((f32[16,32,512]{2,1,0:T(8,128)}), f32[16,32,512]{2,1,0:T(8,128)S(1)}, u32[]{:S(2)}, u32[]{:S(2)}) async-start(f32[16,32,512]{2,1,0:T(8,128)} %bitcast.34), calls=%async_computation.3 | async-start | bytes 2097152 | tf_op jit(solution)/shard_map/all_to_all | solution.py:148
  261.5 25.0 %all-to-all-done.3 = f32[16,32,512]{2,1,0:T(8,128)S(1)} async-done(((f32[16,32,512]{2,1,0:T(8,128)}), f32[16,32,512]{2,1,0:T(8,128)S(1)}, u32[]{:S(2)}, u32[]{:S(2)}) %all-to-all-start.3) | async-done | bytes 1048608 | tf_op jit(solution)/shard_map/all_to_all | solution.py:148
  (112 shorter events, 19.2 us)
Async XLA Ops:
  0.6 14.3 %copy-start.23 = (f32[256,512]{1,0:T(8,128)S(1)}, f32[256,512]{1,0:T(8,128)}, u32[]{:S(2)}) copy-start(f32[256,512]{1,0:T(8,128)} %param.7) | copy-start | bytes 1572868
  1.4 13.6 %collective-permute-start.2 = (f32[1,512]{1,0:T(1,128)S(1)}, f32[1,512]{1,0:T(1,128)S(1)}, u32[]{:S(2)}, u32[]{:S(2)}) collective-permute-start(f32[1,512]{1,0:T(1,128)S(1)} %slice.228), channel_id=1, source_target_pairs={{1,0},{3,2},{5,4},{7,6},{9,8},{11,10},{13,12},{15,14},{17,16},{19,... | collective-permute-start | bytes 6152 | tf_op jit(solution)/shard_map/ppermute | solution.py:20
  3.5 24.0 %collective-permute-start.3 = (f32[2,1,512]{2,1,0:T(1,128)S(1)}, f32[2,1,512]{2,1,0:T(1,128)S(1)}, u32[]{:S(2)}, u32[]{:S(2)}) collective-permute-start(f32[2,1,512]{2,1,0:T(1,128)S(1)} %get-tuple-element.53), channel_id=1, source_target_pairs={{0,1},{2,3},{4,5},{6,7},{8,9},{10,11},{12,13},{14,15},{16,17},{18,... | collective-permute-start | bytes 12296 | tf_op jit(solution)/shard_map/ppermute | solution.py:17
  6.5 21.0 %collective-permute-start.4 = (f32[2,1,512]{2,1,0:T(1,128)S(1)}, f32[2,1,512]{2,1,0:T(1,128)S(1)}, u32[]{:S(2)}, u32[]{:S(2)}) collective-permute-start(f32[2,1,512]{2,1,0:T(1,128)S(1)} %get-tuple-element.54), channel_id=1, source_target_pairs={{1,0},{3,2},{5,4},{7,6},{9,8},{11,10},{13,12},{15,14},{17,16},{19,... | collective-permute-start | bytes 12296 | tf_op jit(solution)/shard_map/ppermute | solution.py:20
  9.9 17.5 %copy-start.25 = (f32[256,512]{1,0:T(8,128)S(1)}, f32[256,512]{1,0:T(8,128)}, u32[]{:S(2)}) copy-start(f32[256,512]{1,0:T(8,128)} %param.6) | copy-start | bytes 1572868
  9.9 17.5 %collective-permute-start = (f32[256,512]{1,0:T(8,128)}, f32[256,512]{1,0:T(8,128)S(1)}, u32[]{:S(2)}, u32[]{:S(2)}) collective-permute-start(f32[256,512]{1,0:T(8,128)} %get-tuple-element.51), channel_id=1, source_target_pairs={{0,2},{2,4},{4,6},{6,8},{8,10},{10,12},{12,14},{1,3},{3,5},{5,7},{... | collective-permute-start | bytes 1572872 | tf_op jit(solution)/shard_map/ppermute | solution.py:28
  15.1 3.6 %collective-permute-start.1 = (f32[1,512]{1,0:T(1,128)S(1)}, f32[1,512]{1,0:T(1,128)S(1)}, u32[]{:S(2)}, u32[]{:S(2)}) collective-permute-start(f32[1,512]{1,0:T(1,128)S(1)} %get-tuple-element.58), channel_id=1, source_target_pairs={{0,1},{2,3},{4,5},{6,7},{8,9},{10,11},{12,13},{14,15},{16,17},{18,... | collective-permute-start | bytes 6152 | tf_op jit(solution)/shard_map/ppermute | solution.py:17
  18.6 8.8 %copy-start.21 = (f32[2,256,512]{2,1,0:T(8,128)S(1)}, f32[2,256,512]{2,1,0:T(8,128)}, u32[]{:S(2)}) copy-start(f32[2,256,512]{2,1,0:T(8,128)} %param.4) | copy-start | bytes 3145732
  18.7 8.8 %copy-start.24 = (f32[2,256,512]{2,1,0:T(8,128)S(1)}, f32[2,256,512]{2,1,0:T(8,128)}, u32[]{:S(2)}) copy-start(f32[2,256,512]{2,1,0:T(8,128)} %param.5) | copy-start | bytes 3145732
  19.1 9.6 %copy-start.2 = (f32[256,512]{1,0:T(8,128)}, f32[256,512]{1,0:T(8,128)S(1)}, u32[]{:S(2)}) copy-start(f32[256,512]{1,0:T(8,128)S(1)} %get-tuple-element.22) | copy-start | bytes 1572868
  19.1 9.6 %copy-start.8 = (f32[256,512]{1,0:T(8,128)}, f32[256,512]{1,0:T(8,128)S(1)}, u32[]{:S(2)}) copy-start(f32[256,512]{1,0:T(8,128)S(1)} %get-tuple-element.23) | copy-start | bytes 1572868
  19.1 9.5 %copy-start.14 = (f32[256,512]{1,0:T(8,128)}, f32[256,512]{1,0:T(8,128)S(1)}, u32[]{:S(2)}) copy-start(f32[256,512]{1,0:T(8,128)S(1)} %get-tuple-element.24) | copy-start | bytes 1572868
  68.2 51.5 %all-to-all-start.1 = ((f32[2,16,32,512]{3,2,0,1:T(8,128)}), f32[2,16,32,512]{3,2,0,1:T(8,128)S(1)}, u32[]{:S(2)}, u32[]{:S(2)}) async-start(f32[2,16,32,512]{3,2,0,1:T(8,128)} %copy.35), calls=%async_computation.1 | async-start | bytes 4194304 | tf_op jit(solution)/shard_map/all_to_all | solution.py:100
  120.0 4.4 %copy-start.20 = (f32[2,2,8,32,512]{4,3,2,1,0:T(8,128)}, f32[2,2,8,32,512]{4,3,2,1,0:T(8,128)S(1)}, u32[]{:S(2)}) copy-start(f32[2,2,8,32,512]{4,3,2,1,0:T(8,128)S(1)} %copy.37) | copy-start | bytes 6291460
  120.0 3.4 %collective-permute-start.5 = (f32[2,2,1,512]{3,2,1,0:T(1,128)S(1)}, f32[2,2,1,512]{3,2,1,0:T(1,128)S(1)}, u32[]{:S(2)}, u32[]{:S(2)}) collective-permute-start(f32[2,2,1,512]{3,2,1,0:T(1,128)S(1)} %get-tuple-element.49), channel_id=1, source_target_pairs={{0,1},{2,3},{4,5},{6,7},{8,9},{10,11},{12,13},{14,15},{16,17},{18,... | collective-permute-start | bytes 24584 | tf_op jit(solution)/shard_map/ppermute | solution.py:17
  121.3 3.1 %collective-permute-start.6 = (f32[2,2,1,512]{3,2,1,0:T(1,128)S(1)}, f32[2,2,1,512]{3,2,1,0:T(1,128)S(1)}, u32[]{:S(2)}, u32[]{:S(2)}) collective-permute-start(f32[2,2,1,512]{3,2,1,0:T(1,128)S(1)} %get-tuple-element.50), channel_id=1, source_target_pairs={{1,0},{3,2},{5,4},{7,6},{9,8},{11,10},{13,12},{15,14},{17,16},{19,... | collective-permute-start | bytes 24584 | tf_op jit(solution)/shard_map/ppermute | solution.py:20
  123.2 1.2 copy-start.3
  123.2 1.2 copy-start.9
  123.2 1.3 copy-start.15
  127.1 4.7 %collective-permute-start.7 = (f32[2,2,1,512]{3,2,1,0:T(1,128)S(1)}, f32[2,2,1,512]{3,2,1,0:T(1,128)S(1)}, u32[]{:S(2)}, u32[]{:S(2)}) collective-permute-start(f32[2,2,1,512]{3,2,1,0:T(1,128)S(1)} %get-tuple-element.45), channel_id=1, source_target_pairs={{0,1},{2,3},{4,5},{6,7},{8,9},{10,11},{12,13},{14,15},{16,17},{18,... | collective-permute-start | bytes 24584 | tf_op jit(solution)/shard_map/ppermute | solution.py:17
  130.1 3.1 %collective-permute-start.8 = (f32[2,2,1,512]{3,2,1,0:T(1,128)S(1)}, f32[2,2,1,512]{3,2,1,0:T(1,128)S(1)}, u32[]{:S(2)}, u32[]{:S(2)}) collective-permute-start(f32[2,2,1,512]{3,2,1,0:T(1,128)S(1)} %get-tuple-element.46), channel_id=1, source_target_pairs={{1,0},{3,2},{5,4},{7,6},{9,8},{11,10},{13,12},{15,14},{17,16},{19,... | collective-permute-start | bytes 24584 | tf_op jit(solution)/shard_map/ppermute | solution.py:20
  141.8 5.4 %copy-start.1 = (f32[2,2,256,512]{3,2,1,0:T(8,128)}, f32[2,2,256,512]{3,2,1,0:T(8,128)S(1)}, u32[]{:S(2)}) copy-start(f32[2,2,256,512]{3,2,1,0:T(8,128)S(1)} %multiply_subtract_fusion.1) | copy-start | bytes 6291460
  141.9 3.8 %collective-permute-start.9 = (f32[2,2,1,512]{3,2,1,0:T(1,128)S(1)}, f32[2,2,1,512]{3,2,1,0:T(1,128)S(1)}, u32[]{:S(2)}, u32[]{:S(2)}) collective-permute-start(f32[2,2,1,512]{3,2,1,0:T(1,128)S(1)} %get-tuple-element.41), channel_id=1, source_target_pairs={{0,1},{2,3},{4,5},{6,7},{8,9},{10,11},{12,13},{14,15},{16,17},{18,... | collective-permute-start | bytes 24584 | tf_op jit(solution)/shard_map/ppermute | solution.py:17
  144.0 3.2 %copy-start.4 = (f32[256,512]{1,0:T(8,128)S(1)}, f32[256,512]{1,0:T(8,128)}, u32[]{:S(2)}) copy-start(f32[256,512]{1,0:T(8,128)} %copy-done.2) | copy-start | bytes 1572868
  144.0 3.2 %copy-start.10 = (f32[256,512]{1,0:T(8,128)S(1)}, f32[256,512]{1,0:T(8,128)}, u32[]{:S(2)}) copy-start(f32[256,512]{1,0:T(8,128)} %copy-done.8) | copy-start | bytes 1572868
  144.0 3.2 %copy-start.16 = (f32[256,512]{1,0:T(8,128)S(1)}, f32[256,512]{1,0:T(8,128)}, u32[]{:S(2)}) copy-start(f32[256,512]{1,0:T(8,128)} %copy-done.14) | copy-start | bytes 1572868
  144.0 3.2 %collective-permute-start.10 = (f32[2,2,1,512]{3,2,1,0:T(1,128)S(1)}, f32[2,2,1,512]{3,2,1,0:T(1,128)S(1)}, u32[]{:S(2)}, u32[]{:S(2)}) collective-permute-start(f32[2,2,1,512]{3,2,1,0:T(1,128)S(1)} %get-tuple-element.42), channel_id=1, source_target_pairs={{1,0},{3,2},{5,4},{7,6},{9,8},{11,10},{13,12},{15,14},{17,16},{19,... | collective-permute-start | bytes 24584 | tf_op jit(solution)/shard_map/ppermute | solution.py:20
  155.3 5.3 %copy-start = (f32[2,2,256,512]{3,2,1,0:T(8,128)}, f32[2,2,256,512]{3,2,1,0:T(8,128)S(1)}, u32[]{:S(2)}) copy-start(f32[2,2,256,512]{3,2,1,0:T(8,128)S(1)} %multiply_add_fusion.2) | copy-start | bytes 6291460
  155.4 3.8 %collective-permute-start.11 = (f32[2,2,1,512]{3,2,1,0:T(1,128)S(1)}, f32[2,2,1,512]{3,2,1,0:T(1,128)S(1)}, u32[]{:S(2)}, u32[]{:S(2)}) collective-permute-start(f32[2,2,1,512]{3,2,1,0:T(1,128)S(1)} %get-tuple-element.37), channel_id=1, source_target_pairs={{0,1},{2,3},{4,5},{6,7},{8,9},{10,11},{12,13},{14,15},{16,17},{18,... | collective-permute-start | bytes 24584 | tf_op jit(solution)/shard_map/ppermute | solution.py:17
  157.4 3.2 %copy-start.5 = (f32[256,512]{1,0:T(8,128)S(1)}, f32[256,512]{1,0:T(8,128)}, u32[]{:S(2)}) copy-start(f32[256,512]{1,0:T(8,128)} %copy-done.2) | copy-start | bytes 1572868
  157.5 3.2 %copy-start.11 = (f32[256,512]{1,0:T(8,128)S(1)}, f32[256,512]{1,0:T(8,128)}, u32[]{:S(2)}) copy-start(f32[256,512]{1,0:T(8,128)} %copy-done.8) | copy-start | bytes 1572868
  157.5 3.2 %copy-start.17 = (f32[256,512]{1,0:T(8,128)S(1)}, f32[256,512]{1,0:T(8,128)}, u32[]{:S(2)}) copy-start(f32[256,512]{1,0:T(8,128)} %copy-done.14) | copy-start | bytes 1572868
  157.5 3.2 %collective-permute-start.12 = (f32[2,2,1,512]{3,2,1,0:T(1,128)S(1)}, f32[2,2,1,512]{3,2,1,0:T(1,128)S(1)}, u32[]{:S(2)}, u32[]{:S(2)}) collective-permute-start(f32[2,2,1,512]{3,2,1,0:T(1,128)S(1)} %get-tuple-element.38), channel_id=1, source_target_pairs={{1,0},{3,2},{5,4},{7,6},{9,8},{11,10},{13,12},{15,14},{17,16},{19,... | collective-permute-start | bytes 24584 | tf_op jit(solution)/shard_map/ppermute | solution.py:20
  169.5 3.8 %collective-permute-start.13 = (f32[2,2,1,512]{3,2,1,0:T(1,128)S(1)}, f32[2,2,1,512]{3,2,1,0:T(1,128)S(1)}, u32[]{:S(2)}, u32[]{:S(2)}) collective-permute-start(f32[2,2,1,512]{3,2,1,0:T(1,128)S(1)} %get-tuple-element.33), channel_id=1, source_target_pairs={{0,1},{2,3},{4,5},{6,7},{8,9},{10,11},{12,13},{14,15},{16,17},{18,... | collective-permute-start | bytes 24584 | tf_op jit(solution)/shard_map/ppermute | solution.py:17
  171.6 3.2 %copy-start.6 = (f32[256,512]{1,0:T(8,128)S(1)}, f32[256,512]{1,0:T(8,128)}, u32[]{:S(2)}) copy-start(f32[256,512]{1,0:T(8,128)} %copy-done.2) | copy-start | bytes 1572868
  171.6 3.2 %copy-start.12 = (f32[256,512]{1,0:T(8,128)S(1)}, f32[256,512]{1,0:T(8,128)}, u32[]{:S(2)}) copy-start(f32[256,512]{1,0:T(8,128)} %copy-done.8) | copy-start | bytes 1572868
  171.6 3.2 %copy-start.18 = (f32[256,512]{1,0:T(8,128)S(1)}, f32[256,512]{1,0:T(8,128)}, u32[]{:S(2)}) copy-start(f32[256,512]{1,0:T(8,128)} %copy-done.14) | copy-start | bytes 1572868
  171.6 3.2 %collective-permute-start.14 = (f32[2,2,1,512]{3,2,1,0:T(1,128)S(1)}, f32[2,2,1,512]{3,2,1,0:T(1,128)S(1)}, u32[]{:S(2)}, u32[]{:S(2)}) collective-permute-start(f32[2,2,1,512]{3,2,1,0:T(1,128)S(1)} %get-tuple-element.34), channel_id=1, source_target_pairs={{1,0},{3,2},{5,4},{7,6},{9,8},{11,10},{13,12},{15,14},{17,16},{19,... | collective-permute-start | bytes 24584 | tf_op jit(solution)/shard_map/ppermute | solution.py:20
  183.6 3.8 %collective-permute-start.15 = (f32[2,2,1,512]{3,2,1,0:T(1,128)S(1)}, f32[2,2,1,512]{3,2,1,0:T(1,128)S(1)}, u32[]{:S(2)}, u32[]{:S(2)}) collective-permute-start(f32[2,2,1,512]{3,2,1,0:T(1,128)S(1)} %get-tuple-element.29), channel_id=1, source_target_pairs={{0,1},{2,3},{4,5},{6,7},{8,9},{10,11},{12,13},{14,15},{16,17},{18,... | collective-permute-start | bytes 24584 | tf_op jit(solution)/shard_map/ppermute | solution.py:17
  185.7 3.2 %copy-start.7 = (f32[256,512]{1,0:T(8,128)S(1)}, f32[256,512]{1,0:T(8,128)}, u32[]{:S(2)}) copy-start(f32[256,512]{1,0:T(8,128)} %copy-done.2) | copy-start | bytes 1572868
  185.7 3.2 %copy-start.13 = (f32[256,512]{1,0:T(8,128)S(1)}, f32[256,512]{1,0:T(8,128)}, u32[]{:S(2)}) copy-start(f32[256,512]{1,0:T(8,128)} %copy-done.8) | copy-start | bytes 1572868
  185.7 3.2 %copy-start.19 = (f32[256,512]{1,0:T(8,128)S(1)}, f32[256,512]{1,0:T(8,128)}, u32[]{:S(2)}) copy-start(f32[256,512]{1,0:T(8,128)} %copy-done.14) | copy-start | bytes 1572868
  185.7 3.2 %collective-permute-start.16 = (f32[2,2,1,512]{3,2,1,0:T(1,128)S(1)}, f32[2,2,1,512]{3,2,1,0:T(1,128)S(1)}, u32[]{:S(2)}, u32[]{:S(2)}) collective-permute-start(f32[2,2,1,512]{3,2,1,0:T(1,128)S(1)} %get-tuple-element.30), channel_id=1, source_target_pairs={{1,0},{3,2},{5,4},{7,6},{9,8},{11,10},{13,12},{15,14},{17,16},{19,... | collective-permute-start | bytes 24584 | tf_op jit(solution)/shard_map/ppermute | solution.py:20
  257.2 29.4 %copy-start.22 = (f32[2,256,512]{2,1,0:T(8,128)S(1)}, f32[2,256,512]{2,1,0:T(8,128)}, u32[]{:S(2)}) copy-start(f32[2,256,512]{2,1,0:T(8,128)} %param.4) | copy-start | bytes 3145732
  257.2 29.3 %all-to-all-start.3 = ((f32[16,32,512]{2,1,0:T(8,128)}), f32[16,32,512]{2,1,0:T(8,128)S(1)}, u32[]{:S(2)}, u32[]{:S(2)}) async-start(f32[16,32,512]{2,1,0:T(8,128)} %bitcast.34), calls=%async_computation.3 | async-start | bytes 2097152 | tf_op jit(solution)/shard_map/all_to_all | solution.py:148
where the time goes:
time: 289 us; the launch traced here: 288 us
  blocking collectives  97.5 us (34%)
  waiting for transfers between devices  90.2 us (31%)
  starting transfers between devices  41.9 us (14%)
  other arithmetic  38 us (13%)
  local copies, waits for them, and re-layouts  13.8 us (5%)
  matrix products  5.1 us (2%)
    all_to_all x1, blocking collectives, shards(): lax.all_to_all(solution, 'tm', split_axis=2, concat_axis=1, tiled=True)  52.6 us
    all_to_all x1, waiting for transfers between devices, shards(): lax.all_to_all(spectrum, 'tm', split_axis=1, concat_axis=2, tiled=True)  47.8 us
    all_to_all x1, blocking collectives, shards(): lax.all_to_all(scaled, 'tm', split_axis=1, concat_axis=0, tiled=True)  32.5 us
    all_to_all x1, waiting for transfers between devices, shards(): lax.all_to_all(correction, 'tm', split_axis=0, concat_axis=1, tiled=True)  25 us
    reduce_sum x6, other arithmetic, freq_norm(): return jnp.sum(values * values, axis=(0, 2, 3))  19 us
    ppermute x8, starting transfers between devices, extended(): lax.ppermute(lax.slice_in_dim(block, block.shape[dim] - width, None, axis...  18.4 us
    psum x5, blocking collectives, reduce_sums(): return lax.psum(values, 'rows')  12.4 us
    ppermute x8, starting transfers between devices, extended(): lax.ppermute(lax.slice_in_dim(block, 0, width, axis=dim), axis, backward)  11 us
  transfers between devices with their start and end apart: 19, of which 10 were waited for; matrix products, arithmetic and copies ran while one was open for 2% of the time, Pallas kernels for 0%

commit v1 on v0

--- a/solution.py
+++ b/solution.py
@@ -145,7 +145,10 @@
         jnp.sin(inverse_angles) / length, flat_imag
     )
     correction = correction.reshape(length, slab_rows, columns_dev)
-    own_steps = lax.all_to_all(correction, "tm", split_axis=0, concat_axis=1, tiled=True)
+    own_steps = jnp.concatenate(
+        lax.all_to_all(jnp.stack(jnp.split(correction, lax.axis_size("tm"), axis=0)), "tm", 0, 0),
+        axis=1,
+    )
     updated = iterate + own_steps / growth[:, None, None]
     return (updated, residual_rms)
 

time: 289 us -> 293 us (1.014)
  local copies, waits for them, and re-layouts: 13.8 us -> 18 us
    unnamed x55 -> x61, local copies, waits for them, and re-layouts: 3.09 us -> 6.27 us
where the time goes in v1:
time: 293 us; the launch traced here: 292 us
  blocking collectives  97.5 us (33%)
  waiting for transfers between devices  90.2 us (31%)
  starting transfers between devices  41.8 us (14%)
  other arithmetic  38 us (13%)
  local copies, waits for them, and re-layouts  18 us (6%)
  matrix products  5.1 us (2%)
    all_to_all x1, blocking collectives, shards(): lax.all_to_all(solution, 'tm', split_axis=2, concat_axis=1, tiled=True)  52.6 us
    all_to_all x1, waiting for transfers between devices, shards(): lax.all_to_all(spectrum, 'tm', split_axis=1, concat_axis=2, tiled=True)  47.7 us
    all_to_all x1, blocking collectives, shards(): lax.all_to_all(scaled, 'tm', split_axis=1, concat_axis=0, tiled=True)  32.5 us
    all_to_all x1, waiting for transfers between devices, shards(): lax.all_to_all(jnp.stack(jnp.split(correction, lax.axis_size('tm'), axis=...  25 us
    reduce_sum x6, other arithmetic, freq_norm(): return jnp.sum(values * values, axis=(0, 2, 3))  19 us
    ppermute x8, starting transfers between devices, extended(): lax.ppermute(lax.slice_in_dim(block, block.shape[dim] - width, None, axis...  18.4 us
    psum x5, blocking collectives, reduce_sums(): return lax.psum(values, 'rows')  12.4 us
    ppermute x8, starting transfers between devices, extended(): lax.ppermute(lax.slice_in_dim(block, 0, width, axis=dim), axis, backward)  11 us
  transfers between devices with their start and end apart: 19, of which 10 were waited for; matrix products, arithmetic and copies ran while one was open for 2% of the time, Pallas kernels for 0%

profile of v1, /device:TPU:0, one launch (start us, length us, event | category | flops | bytes accessed | tf_op | source)
XLA Modules:
  0.0 292.1 jit_solution(7274672574727007025)
XLA Ops:
  3.5 3.0 %collective-permute-start.3 = (f32[2,1,512]{2,1,0:T(1,128)S(1)}, f32[2,1,512]{2,1,0:T(1,128)S(1)}, u32[]{:S(2)}, u32[]{:S(2)}) collective-permute-start(f32[2,1,512]{2,1,0:T(1,128)S(1)} %get-tuple-element.61), channel_id=1, source_target_pairs={{0,1},{2,3},{4,5},{6,7},{8,9},{10,11},{12,13},{14,15},{16,17},{18,... | collective-permute-start | bytes 12296 | tf_op jit(solution)/shard_map/ppermute | solution.py:17
  6.5 1.3 collective-permute-start.4
  7.8 2.1 slice_bitcast_fusion
  9.9 5.1 %collective-permute-start = (f32[256,512]{1,0:T(8,128)}, f32[256,512]{1,0:T(8,128)S(1)}, u32[]{:S(2)}, u32[]{:S(2)}) collective-permute-start(f32[256,512]{1,0:T(8,128)} %get-tuple-element.59), channel_id=1, source_target_pairs={{0,2},{2,4},{4,6},{6,8},{8,10},{10,12},{12,14},{1,3},{3,5},{5,7},{... | collective-permute-start | bytes 1572872 | tf_op jit(solution)/shard_map/ppermute | solution.py:28
  15.1 2.7 collective-permute-start.1
  19.1 8.3 %collective-permute-done = f32[256,512]{1,0:T(8,128)S(1)} collective-permute-done((f32[256,512]{1,0:T(8,128)}, f32[256,512]{1,0:T(8,128)S(1)}, u32[]{:S(2)}, u32[]{:S(2)}) %collective-permute-start) | collective-permute-done | bytes 524320 | tf_op jit(solution)/shard_map/ppermute | solution.py:28
  29.6 32.5 %all_to_all.53 = f32[2,256,512]{2,0,1:T(2,128)S(1)} all-to-all(f32[2,256,512]{2,0,1:T(2,128)S(1)} %copy.31), channel_id=1, replica_groups=mesh['groups'=2,'tm'=8,'rows'=2] {'tm'}, dimensions={1} | all-to-all | bytes 2097152 | tf_op jit(solution)/shard_map/all_to_all | solution.py:92
  62.3 1.5 convolution_bitcast_fusion
  63.8 1.5 convolution_bitcast_fusion.1
  65.7 2.6 copy.35
  68.3 3.6 %all-to-all-start.1 = ((f32[2,16,32,512]{3,2,0,1:T(8,128)}), f32[2,16,32,512]{3,2,0,1:T(8,128)S(1)}, u32[]{:S(2)}, u32[]{:S(2)}) async-start(f32[2,16,32,512]{3,2,0,1:T(8,128)} %copy.35), calls=%async_computation.1 | async-start | bytes 4194304 | tf_op jit(solution)/shard_map/all_to_all | solution.py:100
  72.0 47.7 %all-to-all-done.1 = f32[2,16,32,512]{3,2,0,1:T(8,128)S(1)} async-done(((f32[2,16,32,512]{3,2,0,1:T(8,128)}), f32[2,16,32,512]{3,2,0,1:T(8,128)S(1)}, u32[]{:S(2)}, u32[]{:S(2)}) %all-to-all-start.1) | async-done | bytes 2097184 | tf_op jit(solution)/shard_map/all_to_all | solution.py:100
  121.4 1.3 collective-permute-start.6
  124.6 2.5 multiply_reduce_fusion.4
  127.1 3.0 %collective-permute-start.7 = (f32[2,2,1,512]{3,2,1,0:T(1,128)S(1)}, f32[2,2,1,512]{3,2,1,0:T(1,128)S(1)}, u32[]{:S(2)}, u32[]{:S(2)}) collective-permute-start(f32[2,2,1,512]{3,2,1,0:T(1,128)S(1)} %get-tuple-element.45), channel_id=1, source_target_pairs={{0,1},{2,3},{4,5},{6,7},{8,9},{10,11},{12,13},{14,15},{16,17},{18,... | collective-permute-start | bytes 24584 | tf_op jit(solution)/shard_map/ppermute | solution.py:17
  130.2 1.5 collective-permute-start.8
  131.9 1.3 collective-permute-done.8
  133.2 3.4 %multiply_reduce_fusion.3 = (f32[2]{0:T(128)S(1)}, f32[2,2,256,512]{3,2,1,0:T(8,128)}) fusion(f32[256,512]{1,0:T(8,128)S(1)} %copy-done.15, f32[2,2,256,512]{3,2,1,0:T(8,128)S(1)} %get-tuple-element.19, f32[256,512]{1,0:T(8,128)S(1)} %copy-done.9, f32[2,2,1,512]{3,2,1,0:T(1,128)S(1)} %collective-permute-done.8, f32[256,512]{1,0:T(8,128)S(1)} %copy-done.3, ...), kind=kLoop, calls=%fused_computation.109 | loop fusion | flops 9961470 | bytes 8929304 | tf_op jit(solution)/shard_map/reduce_sum | solution.py:120
  136.6 2.4 all-reduce.8
  139.1 2.8 multiply_subtract_fusion.1
  141.9 2.1 collective-permute-start.9
  144.0 1.4 collective-permute-start.10
  145.7 1.5 collective-permute-done.10
  147.2 3.5 %multiply_reduce_fusion.2 = (f32[2]{0:T(128)S(1)}, f32[2,2,256,512]{3,2,1,0:T(8,128)}) fusion(f32[256,512]{1,0:T(8,128)S(1)} %copy-done.16, f32[2,2,256,512]{3,2,1,0:T(8,128)S(1)} %multiply_subtract_fusion.1, f32[256,512]{1,0:T(8,128)S(1)} %copy-done.10, f32[2,2,1,512]{3,2,1,0:T(1,128)S(1)} %collective-permute-done.10, f32[256,512]{1,0:T(8,128)S(1)} %copy-done.4, ...), kind=kLoop, calls=%fused_computation.107 | loop fusion | flops 9961470 | bytes 8929304 | tf_op jit(solution)/shard_map/reduce_sum | solution.py:120
  150.7 2.4 psum.51
  153.2 2.1 multiply_add_fusion.2
  155.4 2.1 collective-permute-start.11
  157.5 1.4 collective-permute-start.12
  159.2 1.5 collective-permute-done.12
  160.7 3.5 %multiply_reduce_fusion.1 = (f32[2]{0:T(128)S(1)}, f32[2,2,256,512]{3,2,1,0:T(8,128)}) fusion(f32[256,512]{1,0:T(8,128)S(1)} %copy-done.17, f32[2,2,256,512]{3,2,1,0:T(8,128)S(1)} %multiply_add_fusion.2, f32[256,512]{1,0:T(8,128)S(1)} %copy-done.11, f32[2,2,1,512]{3,2,1,0:T(1,128)S(1)} %collective-permute-done.12, f32[256,512]{1,0:T(8,128)S(1)} %copy-done.5, ...), kind=kLoop, calls=%fused_computation.105 | loop fusion | flops 9961470 | bytes 8929304 | tf_op jit(solution)/shard_map/reduce_sum | solution.py:120
  164.3 2.4 psum.52
  166.7 2.8 multiply_subtract_fusion
  169.5 2.1 collective-permute-start.13
  171.6 1.4 collective-permute-start.14
  173.3 1.5 collective-permute-done.14
  174.8 3.5 %multiply_reduce_fusion = (f32[2]{0:T(128)S(1)}, f32[2,2,256,512]{3,2,1,0:T(8,128)}) fusion(f32[256,512]{1,0:T(8,128)S(1)} %copy-done.18, f32[2,2,256,512]{3,2,1,0:T(8,128)S(1)} %multiply_subtract_fusion, f32[256,512]{1,0:T(8,128)S(1)} %copy-done.12, f32[2,2,1,512]{3,2,1,0:T(1,128)S(1)} %collective-permute-done.14, f32[256,512]{1,0:T(8,128)S(1)} %copy-done.6, ...), kind=kLoop, calls=%fused_computation.103 | loop fusion | flops 9961470 | bytes 8929304 | tf_op jit(solution)/shard_map/reduce_sum | solution.py:120
  178.3 2.4 psum.53
  180.8 2.8 multiply_add_fusion.1
  183.6 2.1 collective-permute-start.15
  185.7 1.4 collective-permute-start.16
  187.4 1.5 collective-permute-done.16
  188.9 2.5 fusion.36
  191.4 2.7 all-reduce.7
  194.1 3.1 %multiply_add_fusion = f32[2,2,256,512]{3,2,1,0:T(8,128)S(1)} fusion(f32[2,2,256,512]{3,2,1,0:T(8,128)} %copy-done, f32[2,2,256,512]{3,2,1,0:T(8,128)S(1)} %get-tuple-element.19, f32[2]{0:T(128)S(1)} %div.42, f32[2]{0:T(128)S(1)} %div.40, f32[2]{0:T(128)S(1)} %div.38, f32[2,2,256,512]{3,2,1,0:T(8,128)} %get-tuple-element.11, f32[2]{0:T(128)S(1)} %div.41), kind=kLoop, calls=%fused_computation.101 | loop fusion | flops 3670016 | bytes 8388640 | tf_op jit(solution)/shard_map/add | solution.py:133
  197.1 1.6 copy.40
  198.8 52.6 %all_to_all.54 = f32[2,2,256,512]{3,1,0,2:T(2,128)S(1)} all-to-all(f32[2,2,256,512]{3,1,0,2:T(2,128)S(1)} %copy.40), channel_id=1, replica_groups=mesh['groups'=2,'tm'=8,'rows'=2] {'tm'}, dimensions={2} | all-to-all | bytes 4194304 | tf_op jit(solution)/shard_map/all_to_all | solution.py:140
  261.4 3.8 %all-to-all-start.3 = ((f32[8,2,32,512]{3,2,1,0:T(8,128)}), f32[8,2,32,512]{3,2,1,0:T(8,128)S(1)}, u32[]{:S(2)}, u32[]{:S(2)}) async-start(f32[8,2,32,512]{3,2,1,0:T(8,128)} %bitcast_dynamic-update-slice_fusion), calls=%async_computation.3 | async-start | bytes 2097152 | tf_op jit(solution)/shard_map/all_to_all | solution.py:149
  265.7 25.0 %all-to-all-done.3 = f32[8,2,32,512]{3,2,1,0:T(8,128)S(1)} async-done(((f32[8,2,32,512]{3,2,1,0:T(8,128)}), f32[8,2,32,512]{3,2,1,0:T(8,128)S(1)}, u32[]{:S(2)}, u32[]{:S(2)}) %all-to-all-start.3) | async-done | bytes 1048608 | tf_op jit(solution)/shard_map/all_to_all | solution.py:149
  (120 shorter events, 23.6 us)
Async XLA Ops:
  0.6 14.3 %copy-start.23 = (f32[256,512]{1,0:T(8,128)S(1)}, f32[256,512]{1,0:T(8,128)}, u32[]{:S(2)}) copy-start(f32[256,512]{1,0:T(8,128)} %param.7) | copy-start | bytes 1572868
  1.4 13.6 %collective-permute-start.2 = (f32[1,512]{1,0:T(1,128)S(1)}, f32[1,512]{1,0:T(1,128)S(1)}, u32[]{:S(2)}, u32[]{:S(2)}) collective-permute-start(f32[1,512]{1,0:T(1,128)S(1)} %slice.236), channel_id=1, source_target_pairs={{1,0},{3,2},{5,4},{7,6},{9,8},{11,10},{13,12},{15,14},{17,16},{19,... | collective-permute-start | bytes 6152 | tf_op jit(solution)/shard_map/ppermute | solution.py:20
  3.5 24.0 %collective-permute-start.3 = (f32[2,1,512]{2,1,0:T(1,128)S(1)}, f32[2,1,512]{2,1,0:T(1,128)S(1)}, u32[]{:S(2)}, u32[]{:S(2)}) collective-permute-start(f32[2,1,512]{2,1,0:T(1,128)S(1)} %get-tuple-element.61), channel_id=1, source_target_pairs={{0,1},{2,3},{4,5},{6,7},{8,9},{10,11},{12,13},{14,15},{16,17},{18,... | collective-permute-start | bytes 12296 | tf_op jit(solution)/shard_map/ppermute | solution.py:17
  6.5 21.0 %collective-permute-start.4 = (f32[2,1,512]{2,1,0:T(1,128)S(1)}, f32[2,1,512]{2,1,0:T(1,128)S(1)}, u32[]{:S(2)}, u32[]{:S(2)}) collective-permute-start(f32[2,1,512]{2,1,0:T(1,128)S(1)} %get-tuple-element.62), channel_id=1, source_target_pairs={{1,0},{3,2},{5,4},{7,6},{9,8},{11,10},{13,12},{15,14},{17,16},{19,... | collective-permute-start | bytes 12296 | tf_op jit(solution)/shard_map/ppermute | solution.py:20
  9.9 17.5 %copy-start.25 = (f32[256,512]{1,0:T(8,128)S(1)}, f32[256,512]{1,0:T(8,128)}, u32[]{:S(2)}) copy-start(f32[256,512]{1,0:T(8,128)} %param.6) | copy-start | bytes 1572868
  9.9 17.5 %collective-permute-start = (f32[256,512]{1,0:T(8,128)}, f32[256,512]{1,0:T(8,128)S(1)}, u32[]{:S(2)}, u32[]{:S(2)}) collective-permute-start(f32[256,512]{1,0:T(8,128)} %get-tuple-element.59), channel_id=1, source_target_pairs={{0,2},{2,4},{4,6},{6,8},{8,10},{10,12},{12,14},{1,3},{3,5},{5,7},{... | collective-permute-start | bytes 1572872 | tf_op jit(solution)/shard_map/ppermute | solution.py:28
  15.1 3.6 %collective-permute-start.1 = (f32[1,512]{1,0:T(1,128)S(1)}, f32[1,512]{1,0:T(1,128)S(1)}, u32[]{:S(2)}, u32[]{:S(2)}) collective-permute-start(f32[1,512]{1,0:T(1,128)S(1)} %get-tuple-element.66), channel_id=1, source_target_pairs={{0,1},{2,3},{4,5},{6,7},{8,9},{10,11},{12,13},{14,15},{16,17},{18,... | collective-permute-start | bytes 6152 | tf_op jit(solution)/shard_map/ppermute | solution.py:17
  18.7 8.8 %copy-start.21 = (f32[2,256,512]{2,1,0:T(8,128)S(1)}, f32[2,256,512]{2,1,0:T(8,128)}, u32[]{:S(2)}) copy-start(f32[2,256,512]{2,1,0:T(8,128)} %param.4) | copy-start | bytes 3145732
  18.7 8.8 %copy-start.24 = (f32[2,256,512]{2,1,0:T(8,128)S(1)}, f32[2,256,512]{2,1,0:T(8,128)}, u32[]{:S(2)}) copy-start(f32[2,256,512]{2,1,0:T(8,128)} %param.5) | copy-start | bytes 3145732
  19.1 9.6 %copy-start.2 = (f32[256,512]{1,0:T(8,128)}, f32[256,512]{1,0:T(8,128)S(1)}, u32[]{:S(2)}) copy-start(f32[256,512]{1,0:T(8,128)S(1)} %get-tuple-element.22) | copy-start | bytes 1572868
  19.1 9.6 %copy-start.8 = (f32[256,512]{1,0:T(8,128)}, f32[256,512]{1,0:T(8,128)S(1)}, u32[]{:S(2)}) copy-start(f32[256,512]{1,0:T(8,128)S(1)} %get-tuple-element.23) | copy-start | bytes 1572868
  19.1 9.5 %copy-start.14 = (f32[256,512]{1,0:T(8,128)}, f32[256,512]{1,0:T(8,128)S(1)}, u32[]{:S(2)}) copy-start(f32[256,512]{1,0:T(8,128)S(1)} %get-tuple-element.24) | copy-start | bytes 1572868
  68.3 51.5 %all-to-all-start.1 = ((f32[2,16,32,512]{3,2,0,1:T(8,128)}), f32[2,16,32,512]{3,2,0,1:T(8,128)S(1)}, u32[]{:S(2)}, u32[]{:S(2)}) async-start(f32[2,16,32,512]{3,2,0,1:T(8,128)} %copy.35), calls=%async_computation.1 | async-start | bytes 4194304 | tf_op jit(solution)/shard_map/all_to_all | solution.py:100
  120.0 4.4 %copy-start.20 = (f32[2,2,8,32,512]{4,3,2,1,0:T(8,128)}, f32[2,2,8,32,512]{4,3,2,1,0:T(8,128)S(1)}, u32[]{:S(2)}) copy-start(f32[2,2,8,32,512]{4,3,2,1,0:T(8,128)S(1)} %copy.37) | copy-start | bytes 6291460
  120.1 3.4 %collective-permute-start.5 = (f32[2,2,1,512]{3,2,1,0:T(1,128)S(1)}, f32[2,2,1,512]{3,2,1,0:T(1,128)S(1)}, u32[]{:S(2)}, u32[]{:S(2)}) collective-permute-start(f32[2,2,1,512]{3,2,1,0:T(1,128)S(1)} %get-tuple-element.49), channel_id=1, source_target_pairs={{0,1},{2,3},{4,5},{6,7},{8,9},{10,11},{12,13},{14,15},{16,17},{18,... | collective-permute-start | bytes 24584 | tf_op jit(solution)/shard_map/ppermute | solution.py:17
  121.4 3.1 %collective-permute-start.6 = (f32[2,2,1,512]{3,2,1,0:T(1,128)S(1)}, f32[2,2,1,512]{3,2,1,0:T(1,128)S(1)}, u32[]{:S(2)}, u32[]{:S(2)}) collective-permute-start(f32[2,2,1,512]{3,2,1,0:T(1,128)S(1)} %get-tuple-element.50), channel_id=1, source_target_pairs={{1,0},{3,2},{5,4},{7,6},{9,8},{11,10},{13,12},{15,14},{17,16},{19,... | collective-permute-start | bytes 24584 | tf_op jit(solution)/shard_map/ppermute | solution.py:20
  123.2 1.2 copy-start.3
  123.2 1.2 copy-start.9
  123.3 1.3 copy-start.15
  127.1 4.7 %collective-permute-start.7 = (f32[2,2,1,512]{3,2,1,0:T(1,128)S(1)}, f32[2,2,1,512]{3,2,1,0:T(1,128)S(1)}, u32[]{:S(2)}, u32[]{:S(2)}) collective-permute-start(f32[2,2,1,512]{3,2,1,0:T(1,128)S(1)} %get-tuple-element.45), channel_id=1, source_target_pairs={{0,1},{2,3},{4,5},{6,7},{8,9},{10,11},{12,13},{14,15},{16,17},{18,... | collective-permute-start | bytes 24584 | tf_op jit(solution)/shard_map/ppermute | solution.py:17
  130.2 3.1 %collective-permute-start.8 = (f32[2,2,1,512]{3,2,1,0:T(1,128)S(1)}, f32[2,2,1,512]{3,2,1,0:T(1,128)S(1)}, u32[]{:S(2)}, u32[]{:S(2)}) collective-permute-start(f32[2,2,1,512]{3,2,1,0:T(1,128)S(1)} %get-tuple-element.46), channel_id=1, source_target_pairs={{1,0},{3,2},{5,4},{7,6},{9,8},{11,10},{13,12},{15,14},{17,16},{19,... | collective-permute-start | bytes 24584 | tf_op jit(solution)/shard_map/ppermute | solution.py:20
  141.8 5.4 %copy-start.1 = (f32[2,2,256,512]{3,2,1,0:T(8,128)}, f32[2,2,256,512]{3,2,1,0:T(8,128)S(1)}, u32[]{:S(2)}) copy-start(f32[2,2,256,512]{3,2,1,0:T(8,128)S(1)} %multiply_subtract_fusion.1) | copy-start | bytes 6291460
  141.9 3.8 %collective-permute-start.9 = (f32[2,2,1,512]{3,2,1,0:T(1,128)S(1)}, f32[2,2,1,512]{3,2,1,0:T(1,128)S(1)}, u32[]{:S(2)}, u32[]{:S(2)}) collective-permute-start(f32[2,2,1,512]{3,2,1,0:T(1,128)S(1)} %get-tuple-element.41), channel_id=1, source_target_pairs={{0,1},{2,3},{4,5},{6,7},{8,9},{10,11},{12,13},{14,15},{16,17},{18,... | collective-permute-start | bytes 24584 | tf_op jit(solution)/shard_map/ppermute | solution.py:17
  144.0 3.2 %copy-start.4 = (f32[256,512]{1,0:T(8,128)S(1)}, f32[256,512]{1,0:T(8,128)}, u32[]{:S(2)}) copy-start(f32[256,512]{1,0:T(8,128)} %copy-done.2) | copy-start | bytes 1572868
  144.0 3.2 %copy-start.10 = (f32[256,512]{1,0:T(8,128)S(1)}, f32[256,512]{1,0:T(8,128)}, u32[]{:S(2)}) copy-start(f32[256,512]{1,0:T(8,128)} %copy-done.8) | copy-start | bytes 1572868
  144.0 3.2 %copy-start.16 = (f32[256,512]{1,0:T(8,128)S(1)}, f32[256,512]{1,0:T(8,128)}, u32[]{:S(2)}) copy-start(f32[256,512]{1,0:T(8,128)} %copy-done.14) | copy-start | bytes 1572868
  144.0 3.2 %collective-permute-start.10 = (f32[2,2,1,512]{3,2,1,0:T(1,128)S(1)}, f32[2,2,1,512]{3,2,1,0:T(1,128)S(1)}, u32[]{:S(2)}, u32[]{:S(2)}) collective-permute-start(f32[2,2,1,512]{3,2,1,0:T(1,128)S(1)} %get-tuple-element.42), channel_id=1, source_target_pairs={{1,0},{3,2},{5,4},{7,6},{9,8},{11,10},{13,12},{15,14},{17,16},{19,... | collective-permute-start | bytes 24584 | tf_op jit(solution)/shard_map/ppermute | solution.py:20
  155.3 5.3 %copy-start = (f32[2,2,256,512]{3,2,1,0:T(8,128)}, f32[2,2,256,512]{3,2,1,0:T(8,128)S(1)}, u32[]{:S(2)}) copy-start(f32[2,2,256,512]{3,2,1,0:T(8,128)S(1)} %multiply_add_fusion.2) | copy-start | bytes 6291460
  155.4 3.8 %collective-permute-start.11 = (f32[2,2,1,512]{3,2,1,0:T(1,128)S(1)}, f32[2,2,1,512]{3,2,1,0:T(1,128)S(1)}, u32[]{:S(2)}, u32[]{:S(2)}) collective-permute-start(f32[2,2,1,512]{3,2,1,0:T(1,128)S(1)} %get-tuple-element.37), channel_id=1, source_target_pairs={{0,1},{2,3},{4,5},{6,7},{8,9},{10,11},{12,13},{14,15},{16,17},{18,... | collective-permute-start | bytes 24584 | tf_op jit(solution)/shard_map/ppermute | solution.py:17
  157.5 3.2 %copy-start.5 = (f32[256,512]{1,0:T(8,128)S(1)}, f32[256,512]{1,0:T(8,128)}, u32[]{:S(2)}) copy-start(f32[256,512]{1,0:T(8,128)} %copy-done.2) | copy-start | bytes 1572868
  157.5 3.2 %copy-start.11 = (f32[256,512]{1,0:T(8,128)S(1)}, f32[256,512]{1,0:T(8,128)}, u32[]{:S(2)}) copy-start(f32[256,512]{1,0:T(8,128)} %copy-done.8) | copy-start | bytes 1572868
  157.5 3.2 %copy-start.17 = (f32[256,512]{1,0:T(8,128)S(1)}, f32[256,512]{1,0:T(8,128)}, u32[]{:S(2)}) copy-start(f32[256,512]{1,0:T(8,128)} %copy-done.14) | copy-start | bytes 1572868
  157.5 3.2 %collective-permute-start.12 = (f32[2,2,1,512]{3,2,1,0:T(1,128)S(1)}, f32[2,2,1,512]{3,2,1,0:T(1,128)S(1)}, u32[]{:S(2)}, u32[]{:S(2)}) collective-permute-start(f32[2,2,1,512]{3,2,1,0:T(1,128)S(1)} %get-tuple-element.38), channel_id=1, source_target_pairs={{1,0},{3,2},{5,4},{7,6},{9,8},{11,10},{13,12},{15,14},{17,16},{19,... | collective-permute-start | bytes 24584 | tf_op jit(solution)/shard_map/ppermute | solution.py:20
  169.5 3.8 %collective-permute-start.13 = (f32[2,2,1,512]{3,2,1,0:T(1,128)S(1)}, f32[2,2,1,512]{3,2,1,0:T(1,128)S(1)}, u32[]{:S(2)}, u32[]{:S(2)}) collective-permute-start(f32[2,2,1,512]{3,2,1,0:T(1,128)S(1)} %get-tuple-element.33), channel_id=1, source_target_pairs={{0,1},{2,3},{4,5},{6,7},{8,9},{10,11},{12,13},{14,15},{16,17},{18,... | collective-permute-start | bytes 24584 | tf_op jit(solution)/shard_map/ppermute | solution.py:17
  171.6 3.2 %copy-start.6 = (f32[256,512]{1,0:T(8,128)S(1)}, f32[256,512]{1,0:T(8,128)}, u32[]{:S(2)}) copy-start(f32[256,512]{1,0:T(8,128)} %copy-done.2) | copy-start | bytes 1572868
  171.6 3.2 %copy-start.12 = (f32[256,512]{1,0:T(8,128)S(1)}, f32[256,512]{1,0:T(8,128)}, u32[]{:S(2)}) copy-start(f32[256,512]{1,0:T(8,128)} %copy-done.8) | copy-start | bytes 1572868
  171.6 3.2 %copy-start.18 = (f32[256,512]{1,0:T(8,128)S(1)}, f32[256,512]{1,0:T(8,128)}, u32[]{:S(2)}) copy-start(f32[256,512]{1,0:T(8,128)} %copy-done.14) | copy-start | bytes 1572868
  171.6 3.2 %collective-permute-start.14 = (f32[2,2,1,512]{3,2,1,0:T(1,128)S(1)}, f32[2,2,1,512]{3,2,1,0:T(1,128)S(1)}, u32[]{:S(2)}, u32[]{:S(2)}) collective-permute-start(f32[2,2,1,512]{3,2,1,0:T(1,128)S(1)} %get-tuple-element.34), channel_id=1, source_target_pairs={{1,0},{3,2},{5,4},{7,6},{9,8},{11,10},{13,12},{15,14},{17,16},{19,... | collective-permute-start | bytes 24584 | tf_op jit(solution)/shard_map/ppermute | solution.py:20
  183.6 3.8 %collective-permute-start.15 = (f32[2,2,1,512]{3,2,1,0:T(1,128)S(1)}, f32[2,2,1,512]{3,2,1,0:T(1,128)S(1)}, u32[]{:S(2)}, u32[]{:S(2)}) collective-permute-start(f32[2,2,1,512]{3,2,1,0:T(1,128)S(1)} %get-tuple-element.29), channel_id=1, source_target_pairs={{0,1},{2,3},{4,5},{6,7},{8,9},{10,11},{12,13},{14,15},{16,17},{18,... | collective-permute-start | bytes 24584 | tf_op jit(solution)/shard_map/ppermute | solution.py:17
  185.7 3.2 %copy-start.7 = (f32[256,512]{1,0:T(8,128)S(1)}, f32[256,512]{1,0:T(8,128)}, u32[]{:S(2)}) copy-start(f32[256,512]{1,0:T(8,128)} %copy-done.2) | copy-start | bytes 1572868
  185.7 3.2 %copy-start.13 = (f32[256,512]{1,0:T(8,128)S(1)}, f32[256,512]{1,0:T(8,128)}, u32[]{:S(2)}) copy-start(f32[256,512]{1,0:T(8,128)} %copy-done.8) | copy-start | bytes 1572868
  185.7 3.2 %copy-start.19 = (f32[256,512]{1,0:T(8,128)S(1)}, f32[256,512]{1,0:T(8,128)}, u32[]{:S(2)}) copy-start(f32[256,512]{1,0:T(8,128)} %copy-done.14) | copy-start | bytes 1572868
  185.7 3.2 %collective-permute-start.16 = (f32[2,2,1,512]{3,2,1,0:T(1,128)S(1)}, f32[2,2,1,512]{3,2,1,0:T(1,128)S(1)}, u32[]{:S(2)}, u32[]{:S(2)}) collective-permute-start(f32[2,2,1,512]{3,2,1,0:T(1,128)S(1)} %get-tuple-element.30), channel_id=1, source_target_pairs={{1,0},{3,2},{5,4},{7,6},{9,8},{11,10},{13,12},{15,14},{17,16},{19,... | collective-permute-start | bytes 24584 | tf_op jit(solution)/shard_map/ppermute | solution.py:20
  261.4 29.4 %copy-start.22 = (f32[2,256,512]{2,1,0:T(8,128)S(1)}, f32[2,256,512]{2,1,0:T(8,128)}, u32[]{:S(2)}) copy-start(f32[2,256,512]{2,1,0:T(8,128)} %param.4) | copy-start | bytes 3145732
  261.4 29.3 %all-to-all-start.3 = ((f32[8,2,32,512]{3,2,1,0:T(8,128)}), f32[8,2,32,512]{3,2,1,0:T(8,128)S(1)}, u32[]{:S(2)}, u32[]{:S(2)}) async-start(f32[8,2,32,512]{3,2,1,0:T(8,128)} %bitcast_dynamic-update-slice_fusion), calls=%async_computation.3 | async-start | bytes 2097152 | tf_op jit(solution)/shard_map/all_to_all | solution.py:149
